TPU v7x, 128 devices: a whole 4x4x4 slice. The times are simulated.
128 devices in a mesh: geo: 8 (over x, core), dist: 16 (over z, y).
Axes of the slice: x: 4, y: 4, z: 4, core: 2. Of those that a mesh axis runs over, the one named last changes fastest.
Arguments:
- estimates: bfloat16 [6144, 7424], P(('geo', 'dist')), may hold values from -4 to 4
- factors: bfloat16 [6144, 7424], P(('geo', 'dist')), may hold values from -0.625 to 0.625
- variances: bfloat16 [6144, 116], P(('geo', 'dist')), may hold values from 0.019897461 to 0.5
- intersection_tracts: int32 [2048, 32], P('dist'), may hold values from 0 to 6143, as said below
- intersection_weights: int32 [2048, 32], P('dist'), may hold values from 1 to 256
Outputs:
- marginal: float32 [2048, 7424], P('dist')
- covariance: float32 [2048, 13456], P('dist')
Inputs may be any that keep to these rules, and one draw needn't show every extreme that they name: `intersection_tracts`: each district's intersections are 32 different tracts among 64 consecutive ones, counted cyclically over the region.
All inputs are finite; a program needn't handle non-finite values.
Results may differ from a plain program's by a relative error of at most 0.0003.
Values may be sent and summed in bfloat16 or wider, within the bound.
A program may use at most 128 MiB of HBM per device.

v0:
```python
import jax
import jax.numpy as jnp
from jax import lax
from jax.sharding import PartitionSpec as P


def assemble(est_sum, fac_sum, var_sum):
    count = est_sum.shape[0]
    ages = var_sum.shape[1]
    shaped = fac_sum.reshape(count, ages, fac_sum.shape[1] // ages)
    outer = jnp.einsum("dik,djk->dij", shaped, shaped, precision=lax.Precision.HIGHEST)
    outer = outer + var_sum[:, :, None] * jnp.eye(ages, dtype=jnp.float32)[None, :, :]
    return (est_sum, outer.reshape(count, ages * ages))


def shards(estimates, factors, variances, intersection_tracts, intersection_weights):
    geo_index = lax.axis_index("geo")
    block = estimates.shape[0] * lax.axis_size("dist")
    local_ids = intersection_tracts - geo_index * block
    positions = jnp.arange(block, dtype=jnp.int32)
    onehot = (local_ids[:, :, None] == positions[None, None, :]).astype(jnp.float32)
    share = intersection_weights.astype(jnp.float32) / 256.0
    weight_mat = jnp.sum(onehot * share[:, :, None], axis=1).astype(jnp.bfloat16)
    square_mat = jnp.sum(onehot * (share * share)[:, :, None], axis=1)
    est_new = jnp.dot(
        weight_mat,
        lax.all_gather(estimates, "dist", axis=0, tiled=True),
        preferred_element_type=jnp.float32,
    )
    fac_new = jnp.dot(
        weight_mat,
        lax.all_gather(factors, "dist", axis=0, tiled=True),
        preferred_element_type=jnp.float32,
    )
    var_new = jnp.dot(
        square_mat,
        lax.all_gather(variances, "dist", axis=0, tiled=True).astype(jnp.float32),
        precision=lax.Precision.HIGHEST,
    )
    est_sum, fac_sum, var_sum = lax.psum((est_new, fac_new, var_new), "geo")
    return assemble(est_sum, fac_sum, var_sum)


def solution(mesh):
    return jax.shard_map(
        shards,
        mesh=mesh,
        in_specs=(
            P(("geo", "dist"), None),
            P(("geo", "dist"), None),
            P(("geo", "dist"), None),
            P("dist", None),
            P("dist", None),
        ),
        out_specs=(P("dist", None), P("dist", None)),
        check_vma=False,
    )
```

profile of v0, /device:TPU:1, one launch (start us, length us, event | category | flops | bytes accessed | tf_op | source)
XLA Modules:
  0.0 340.1 jit_solution(11527298273313712709)
XLA Ops:
  7.2 0.0 all-gather.5.cloned.1.call-start
  7.2 0.7 all-gather.5.cloned.1.call-update
  7.9 0.0 all-gather.3.cloned.1.call-start
  7.9 0.7 all-gather.3.cloned.1.call-update
  8.6 0.0 all-reduce.3.cloned.1.call-start
  8.7 0.7 convert_multiply_fusion
  9.4 0.1 copy.24
  9.5 0.7 broadcast_subtract_fusion
  10.2 0.1 copy.20
  10.3 0.1 copy.21
  10.4 13.2 %select_reduce_fusion = (f32[128,768]{1,0:T(8,128)S(1)}, bf16[128,768]{1,0:T(8,128)(2,1)S(1)}) fusion(f32[128,32]{1,0:T(8,128)S(1)} %copy.24, s32[128,32]{1,0:T(8,128)S(1)} %copy.20, f32[128,32]{1,0:T(8,128)S(1)} %copy.21), kind=kLoop, calls=%fused_computation | loop fusion | flops 15532032 | bytes 638976 | tf_op jit(solution)/shard_map/reduce_sum | solution.py:24
  23.6 74.5 %all-gather.5.cloned.1.call-done = bf16[768,7424]{1,0:T(8,128)(2,1)} async-done(((bf16[48,7424]{1,0:T(8,128)(2,1)}), bf16[768,7424]{1,0:T(8,128)(2,1)}) %all-gather.5.cloned.1.call-update) | async-done | bytes 11403280 | tf_op jit(solution)/shard_map/all_gather | solution.py:32
  98.1 10.6 %fusion.7 = f32[128,7424]{0,1:T(8,128)} fusion(bf16[128,768]{1,0:T(8,128)(2,1)S(1)} %get-tuple-element.5, bf16[768,7424]{1,0:T(8,128)(2,1)} %all-gather.5.cloned.1.call-done), kind=kOutput, calls=%fused_computation.14 | convolution fusion | flops 1459617792 | bytes 15400960 | tf_op jit(solution)/shard_map/dot_general | solution.py:30
  108.7 5.4 %copy.23 = f32[128,116,64]{1,2,0:T(8,128)} copy(f32[128,116,64]{0,2,1:T(8,128)} %bitcast.9) | data formatting | bytes 7602176 | tf_op jit(solution)/shard_map/reshape | solution.py:10
  114.2 0.0 copy-start
  114.2 70.4 %all-gather.3.cloned.1.call-done = bf16[768,7424]{1,0:T(8,128)(2,1)} async-done(((bf16[48,7424]{1,0:T(8,128)(2,1)}), bf16[768,7424]{1,0:T(8,128)(2,1)}) %all-gather.3.cloned.1.call-update) | async-done | bytes 11403280 | tf_op jit(solution)/shard_map/all_gather | solution.py:27
  184.5 7.8 %fusion.8 = f32[128,7424]{1,0:T(8,128)} fusion(bf16[128,768]{1,0:T(8,128)(2,1)S(1)} %get-tuple-element.5, bf16[768,7424]{1,0:T(8,128)(2,1)} %all-gather.3.cloned.1.call-done), kind=kOutput, calls=%fused_computation.15 | convolution fusion | flops 1459617792 | bytes 15400960 | tf_op jit(solution)/shard_map/dot_general | solution.py:25
  192.3 0.0 all-reduce.3.cloned.1.call-update
  192.3 0.0 copy-done
  192.3 19.1 %all_gather.11 = bf16[768,116]{1,0:T(8,128)(2,1)S(1)} all-gather(bf16[48,116]{1,0:T(8,128)(2,1)S(1)} %copy-done), channel_id=1, replica_groups=mesh['geo'=8,'dist'=16] {'dist'}, dimensions={0}, use_global_device_ids=true | all-gather | bytes 189312 | tf_op jit(solution)/shard_map/all_gather | solution.py:37
  211.5 0.4 fusion.6
  211.9 27.8 %psum.23 = f32[128,116]{0,1:T(8,128)S(1)} all-reduce(f32[128,116]{0,1:T(8,128)S(1)} %fusion.6), channel_id=1, replica_groups=mesh['geo'=8,'dist'=16] {'geo'}, use_global_device_ids=true, to_apply=%region_4.0 | all-reduce | flops 14848 | bytes 118784 | tf_op jit(solution)/shard_map/psum | solution.py:40
  239.6 0.1 copy.25
  239.7 52.9 %all-reduce.3.cloned.1.call-done = (f32[128,7424]{1,0:T(8,128)}, f32[128,116,64]{1,2,0:T(8,128)}) async-done(((f32[128,7424]{1,0:T(8,128)}, f32[128,116,64]{1,2,0:T(8,128)}), (f32[128,7424]{1,0:T(8,128)}, f32[128,116,64]{1,2,0:T(8,128)})) %all-reduce.3.cloned.1.call-update) | async-done | bytes 7602192 | tf_op jit(solution)/shard_map/psum | solution.py:40
  292.6 20.0 %multiply_add_fusion = f32[128,116,116]{2,1,0:T(8,128)} fusion(f32[116,116]{1,0:T(8,128)S(1)} %fusion.4, f32[128,116]{1,0:T(8,128)S(1)} %copy.25, f32[128,116,64]{1,2,0:T(8,128)} %get-tuple-element.7), kind=kOutput, calls=%fused_computation.3 | convolution fusion | flops 1326223360 | bytes 10803776 | tf_op jit(solution)/shard_map/dik,djk->dij/dot_general | solution.py:11
  312.6 8.5 %reshape.24 = f32[128,13456]{1,0:T(8,128)} reshape(f32[128,116,116]{2,1,0:T(8,128)} %multiply_add_fusion) | data formatting | bytes 13778944 | tf_op jit(solution)/shard_map/reshape | solution.py:13
  321.2 8.2 %copy.28 = f32[128,13456]{0,1:T(8,128)} copy(f32[128,13456]{1,0:T(8,128)} %reshape.24) | data formatting | bytes 13778944 | tf_op jit(solution)/shard_map/reshape | solution.py:13
  329.4 4.2 %copy.31 = f32[128,7424]{1,0:T(8,128)} copy(f32[128,7424]{1,0:T(8,128)} %get-tuple-element.10) | data formatting | bytes 7602176
  (1 shorter events, 0.0 us)
Async XLA Ops:
  7.2 90.9 %all-gather.5.cloned.1.call-start = ((), (), s32[]{:S(2)}) async-start(), calls=%async_computation.1 | async-start | bytes 12115968 | tf_op jit(solution)/shard_map/all_gather | solution.py:32
  7.9 176.6 %all-gather.3.cloned.1.call-start = ((), (), s32[]{:S(2)}) async-start(), calls=%async_computation | async-start | bytes 12115968 | tf_op jit(solution)/shard_map/all_gather | solution.py:27
  8.6 284.0 %all-reduce.3.cloned.1.call-start = ((), (), s32[]{:S(2)}) async-start(), calls=%async_computation.2 | async-start | bytes 15990784 | tf_op jit(solution)/shard_map/psum | solution.py:40
  114.2 78.2 %copy-start = (bf16[48,116]{1,0:T(8,128)(2,1)S(1)}, bf16[48,116]{1,0:T(8,128)(2,1)}, u32[]{:S(2)}) copy-start(bf16[48,116]{1,0:T(8,128)(2,1)} %param.7) | copy-start | bytes 33412
Sparse Core Ops, SparseCore 0:
  10.1 87.8 all-gather.4
  100.2 84.2 all-gather.2
  192.5 100.1 all-reduce.2
where the time goes:
time: 341 us; the launch traced here: 340 us
  waiting for transfers between devices  199 us (58%)
  blocking collectives  46.9 us (14%)
  matrix products  38.8 us (11%)
  local copies, waits for them, and re-layouts  26.8 us (8%)
  other arithmetic  14.6 us (4%)
  between operations  13.8 us (4%)
    all_gather x1, waiting for transfers between devices, shards(): lax.all_gather(factors, 'dist', axis=0, tiled=True)  74.5 us
    all_gather x1, waiting for transfers between devices, shards(): lax.all_gather(estimates, 'dist', axis=0, tiled=True)  70.4 us
    psum x1, waiting for transfers between devices, shards(): est_sum, fac_sum, var_sum = lax.psum((est_new, fac_new, var_new), 'geo')  52.9 us
    psum x1, blocking collectives, shards(): est_sum, fac_sum, var_sum = lax.psum((est_new, fac_new, var_new), 'geo')  27.8 us
    dot_general x1, matrix products, assemble(): jnp.einsum('dik,djk->dij', shaped, shaped, precision=lax.Precision.HIGHEST)  20 us
    all_gather x1, blocking collectives, shards(): lax.all_gather(variances, 'dist', axis=0, tiled=True).astype(jnp.float32)  19.1 us
    reshape x2, local copies, waits for them, and re-layouts, assemble(): return (est_sum, outer.reshape(count, ages * ages))  16.8 us
    reduce_sum x1, other arithmetic, shards(): square_mat = jnp.sum(onehot * (share * share)[:, :, None], axis=1)  13.2 us
  transfers between devices with their start and end apart: 3, of which 3 were waited for; matrix products, arithmetic and copies ran while one was open for 9% of the time, Pallas kernels for 0%

commit v1 on v0

--- a/solution.py
+++ b/solution.py
@@ -29,7 +29,9 @@
     )
     fac_new = jnp.dot(
         weight_mat,
-        lax.all_gather(factors, "dist", axis=0, tiled=True),
+        jnp.concatenate(
+            lax.all_to_all(jnp.stack([factors] * lax.axis_size("dist")), "dist", 0, 0), axis=0
+        ),
         preferred_element_type=jnp.float32,
     )
     var_new = jnp.dot(

time: 341 us -> 404 us (1.18)
  waiting for transfers between devices: 199 us -> 247 us
  starting transfers between devices: 0.11 us -> 8.85 us
  local copies, waits for them, and re-layouts: 26.8 us -> 32.6 us
    all_to_all x0 -> x1, waiting for transfers between devices: none -> 192 us  [shards(): lax.all_to_all(jnp.stack([factors] * lax.axis_size('dist')), 'dist', 0, 0)]
    all_gather x1 -> x0, waiting for transfers between devices: 74.5 us -> none  [shards(): lax.all_gather(factors, 'dist', axis=0, tiled=True)]
    all_gather x1, waiting for transfers between devices: 70.4 us -> 0.01 us  [shards(): lax.all_gather(estimates, 'dist', axis=0, tiled=True)]
    all_to_all x0 -> x1, starting transfers between devices: none -> 8.77 us  [shards(): lax.all_to_all(jnp.stack([factors] * lax.axis_size('dist')), 'dist', 0, 0)]
    another operation x0 -> x1, local copies, waits for them, and re-layouts: none -> 5.99 us  [shards(): jnp.stack([factors] * lax.axis_size('dist'))]
  transfers between devices with their start and end apart: 3 -> 3, of which waited for: 3 -> 2; matrix products, arithmetic and copies ran while one was open for 9% -> 9% of each run, Pallas kernels for 0% -> 0%
where the time goes in v1:
time: 404 us
  waiting for transfers between devices  247 us (61%)
  blocking collectives  49.7 us (12%)
  matrix products  38.8 us (10%)
  local copies, waits for them, and re-layouts  32.6 us (8%)
  between operations  14.1 us (3%)
  other arithmetic  13.2 us (3%)
  starting transfers between devices  8.85 us (2%)
    all_to_all x1, waiting for transfers between devices, shards(): lax.all_to_all(jnp.stack([factors] * lax.axis_size('dist')), 'dist', 0, 0)  192 us
    psum x1, waiting for transfers between devices, shards(): est_sum, fac_sum, var_sum = lax.psum((est_new, fac_new, var_new), 'geo')  53.8 us
    psum x1, blocking collectives, shards(): est_sum, fac_sum, var_sum = lax.psum((est_new, fac_new, var_new), 'geo')  27.7 us
    all_gather x1, blocking collectives, shards(): lax.all_gather(variances, 'dist', axis=0, tiled=True).astype(jnp.float32)  22 us
    dot_general x1, matrix products, assemble(): jnp.einsum('dik,djk->dij', shaped, shaped, precision=lax.Precision.HIGHEST)  20 us
    reshape x2, local copies, waits for them, and re-layouts, assemble(): return (est_sum, outer.reshape(count, ages * ages))  16.7 us
    reduce_sum x1, other arithmetic, shards(): square_mat = jnp.sum(onehot * (share * share)[:, :, None], axis=1)  13.2 us
    dot_general x1, matrix products, shards(): jnp.dot(weight_mat, jnp.concatenate(lax.all_to_all(jnp.stack([factors] *...  10.6 us
  transfers between devices with their start and end apart: 3, of which 2 were waited for; matrix products, arithmetic and copies ran while one was open for 9% of the time, Pallas kernels for 0%

profile of v1, /device:TPU:1, one launch (start us, length us, event | category | flops | bytes accessed | tf_op | source)
XLA Modules:
  0.0 403.7 jit_solution(14390370973777757755)
XLA Ops:
  7.2 0.0 all-gather.2.cloned.1.call-start
  7.2 0.7 all-gather.2.cloned.1.call-update
  7.9 6.0 %stack.2 = bf16[16,48,7424]{2,1,0:T(8,128)(2,1)} broadcast(bf16[48,7424]{1,0:T(8,128)(2,1)} %param.6), dimensions={1,2} | broadcast | bytes 12115968 | tf_op jit(solution)/shard_map/stack | solution.py:33
  13.9 0.0 copy-start
  13.9 0.0 copy-start.1
  13.9 8.8 %all-to-all-start = ((bf16[16,48,7424]{2,1,0:T(8,128)(2,1)}), bf16[16,48,7424]{2,1,0:T(8,128)(2,1)}, u32[]{:S(2)}, u32[]{:S(2)}) async-start(bf16[16,48,7424]{2,1,0:T(8,128)(2,1)} %stack.2), calls=%async_computation | async-start | bytes 22806528 | tf_op jit(solution)/shard_map/all_to_all | solution.py:33
  22.7 0.0 all-reduce.3.cloned.1.call-start
  22.7 0.0 copy-done
  22.7 0.1 copy.21
  22.8 0.1 copy.24
  22.9 0.0 copy-done.1
  23.0 0.1 copy.20
  23.1 13.2 %select_reduce_fusion = (f32[128,768]{1,0:T(8,128)S(1)}, bf16[128,768]{1,0:T(8,128)(2,1)S(1)}) fusion(f32[128,32]{1,0:T(8,128)S(1)} %copy.24, s32[128,32]{1,0:T(8,128)S(1)} %copy.20, f32[128,32]{1,0:T(8,128)S(1)} %copy.21), kind=kLoop, calls=%fused_computation | loop fusion | flops 15532032 | bytes 638976 | tf_op jit(solution)/shard_map/reduce_sum | solution.py:24
  36.2 192.0 %all-to-all-done = bf16[16,48,7424]{2,1,0:T(8,128)(2,1)} async-done(((bf16[16,48,7424]{2,1,0:T(8,128)(2,1)}), bf16[16,48,7424]{2,1,0:T(8,128)(2,1)}, u32[]{:S(2)}, u32[]{:S(2)}) %all-to-all-start) | async-done | bytes 11403296 | tf_op jit(solution)/shard_map/all_to_all | solution.py:33
  228.3 10.6 %fusion.7 = f32[128,7424]{0,1:T(8,128)} fusion(bf16[128,768]{1,0:T(8,128)(2,1)S(1)} %get-tuple-element.5, bf16[768,7424]{1,0:T(8,128)(2,1)} %bitcast), kind=kOutput, calls=%fused_computation.14 | convolution fusion | flops 1459617792 | bytes 15400960 | tf_op jit(solution)/shard_map/dot_general | solution.py:30
  238.9 5.3 %copy.23 = f32[128,116,64]{1,2,0:T(8,128)} copy(f32[128,116,64]{0,2,1:T(8,128)} %bitcast.10) | data formatting | bytes 7602176 | tf_op jit(solution)/shard_map/reshape | solution.py:10
  244.2 0.0 copy-start.2
  244.2 0.0 all-gather.2.cloned.1.call-done
  244.2 7.8 %fusion.8 = f32[128,7424]{1,0:T(8,128)} fusion(bf16[128,768]{1,0:T(8,128)(2,1)S(1)} %get-tuple-element.5, bf16[768,7424]{1,0:T(8,128)(2,1)} %all-gather.2.cloned.1.call-done), kind=kOutput, calls=%fused_computation.15 | convolution fusion | flops 1459617792 | bytes 15400960 | tf_op jit(solution)/shard_map/dot_general | solution.py:25
  252.0 0.0 all-reduce.3.cloned.1.call-update
  252.0 0.0 copy-done.2
  252.0 22.0 %all_gather.7 = bf16[768,116]{1,0:T(8,128)(2,1)S(1)} all-gather(bf16[48,116]{1,0:T(8,128)(2,1)S(1)} %copy-done.2), channel_id=1, replica_groups=mesh['geo'=8,'dist'=16] {'dist'}, dimensions={0}, use_global_device_ids=true | all-gather | bytes 189312 | tf_op jit(solution)/shard_map/all_gather | solution.py:39
  274.0 0.4 fusion.6
  274.4 27.7 %psum.23 = f32[128,116]{0,1:T(8,128)S(1)} all-reduce(f32[128,116]{0,1:T(8,128)S(1)} %fusion.6), channel_id=1, replica_groups=mesh['geo'=8,'dist'=16] {'geo'}, use_global_device_ids=true, to_apply=%region_4.0 | all-reduce | flops 14848 | bytes 118784 | tf_op jit(solution)/shard_map/psum | solution.py:42
  302.0 0.1 copy.25
  302.2 53.8 %all-reduce.3.cloned.1.call-done = (f32[128,7424]{1,0:T(8,128)}, f32[128,116,64]{1,2,0:T(8,128)}) async-done(((f32[128,7424]{1,0:T(8,128)}, f32[128,116,64]{1,2,0:T(8,128)}), (f32[128,7424]{1,0:T(8,128)}, f32[128,116,64]{1,2,0:T(8,128)})) %all-reduce.3.cloned.1.call-update) | async-done | bytes 7602192 | tf_op jit(solution)/shard_map/psum | solution.py:42
  355.9 20.0 %multiply_add_fusion = f32[128,116,116]{2,1,0:T(8,128)} fusion(f32[116,116]{1,0:T(8,128)S(1)} %fusion.4, f32[128,116]{1,0:T(8,128)S(1)} %copy.25, f32[128,116,64]{1,2,0:T(8,128)} %get-tuple-element.7), kind=kOutput, calls=%fused_computation.3 | convolution fusion | flops 1326223360 | bytes 10803776 | tf_op jit(solution)/shard_map/dik,djk->dij/dot_general | solution.py:11
  375.9 8.5 %reshape.30 = f32[128,13456]{1,0:T(8,128)} reshape(f32[128,116,116]{2,1,0:T(8,128)} %multiply_add_fusion) | data formatting | bytes 13778944 | tf_op jit(solution)/shard_map/reshape | solution.py:13
  384.5 8.2 %copy.28 = f32[128,13456]{0,1:T(8,128)} copy(f32[128,13456]{1,0:T(8,128)} %reshape.30) | data formatting | bytes 13778944 | tf_op jit(solution)/shard_map/reshape | solution.py:13
  392.7 4.2 %copy.31 = f32[128,7424]{1,0:T(8,128)} copy(f32[128,7424]{1,0:T(8,128)} %get-tuple-element.10) | data formatting | bytes 7602176
  (3 shorter events, 0.0 us)
Async XLA Ops:
  7.2 237.0 %all-gather.2.cloned.1.call-start = ((), (), s32[]{:S(2)}) async-start(), calls=%async_computation.1 | async-start | bytes 12115968 | tf_op jit(solution)/shard_map/all_gather | solution.py:27
  13.9 8.8 %copy-start = (s32[128,32]{0,1:T(8,128)S(1)}, s32[128,32]{0,1:T(8,128)}, u32[]{:S(2)}) copy-start(s32[128,32]{0,1:T(8,128)} %param.9) | copy-start | bytes 49156
  13.9 9.1 %copy-start.1 = (s32[128,32]{0,1:T(8,128)S(1)}, s32[128,32]{0,1:T(8,128)}, u32[]{:S(2)}) copy-start(s32[128,32]{0,1:T(8,128)} %param.8) | copy-start | bytes 49156
  13.9 214.4 %all-to-all-start = ((bf16[16,48,7424]{2,1,0:T(8,128)(2,1)}), bf16[16,48,7424]{2,1,0:T(8,128)(2,1)}, u32[]{:S(2)}, u32[]{:S(2)}) async-start(bf16[16,48,7424]{2,1,0:T(8,128)(2,1)} %stack.2), calls=%async_computation | async-start | bytes 22806528 | tf_op jit(solution)/shard_map/all_to_all | solution.py:33
  22.7 333.3 %all-reduce.3.cloned.1.call-start = ((), (), s32[]{:S(2)}) async-start(), calls=%async_computation.2 | async-start | bytes 15990784 | tf_op jit(solution)/shard_map/psum | solution.py:42
  244.2 7.8 %copy-start.2 = (bf16[48,116]{1,0:T(8,128)(2,1)S(1)}, bf16[48,116]{1,0:T(8,128)(2,1)}, u32[]{:S(2)}) copy-start(bf16[48,116]{1,0:T(8,128)(2,1)} %param.7) | copy-start | bytes 33412
Sparse Core Ops, SparseCore 0:
  10.1 230.5 all-gather.1
  252.1 103.7 all-reduce.2
